TPU v7x, 32 devices: a whole 2x2x4 slice. The times are simulated.
32 devices in a mesh: row: 4 (over z), col: 8 (over y, x, core).
Axes of the slice: x: 2, y: 2, z: 4, core: 2. Of those that a mesh axis runs over, the one named last changes fastest.
Arguments:
- amplitudes: bfloat16 [2048, 8192], P(('col', 'row')), may hold values from -6 to 6
- integrals: bfloat16 [8192, 8192], P('row', 'col'), may hold values from -0.0625 to 0.0625
- integral_tiles: int32 [64, 64], P('row', 'col'), may hold values from 0 to 1, as said below
- amplitude_tiles: int32 [16, 64], P('col'), may hold values 0 or 1
Outputs:
- ladder: float32 [2048, 8192], P('col', 'row')
Inputs may be any that keep to these rules, and one draw needn't show every extreme that they name: `integral_tiles`: tiles of higher ab index are more often nonzero.
All inputs are finite; a program needn't handle non-finite values. No bound on the sum of `amplitude_tiles` on one device may be relied on, other than what follows from the above.
Results may differ from a plain program's by a relative error of at most 0.0003.
Values may be sent and summed in bfloat16 or wider, within the bound.
No kernel may reach another device: no remote copies, remote signals or barrier semaphores. Data moves between devices by JAX's collectives and lax.ppermute only.
A program may use at most 128 MiB of HBM per device.

v0:
```python
import jax
import jax.numpy as jnp
from jax import lax
from jax.sharding import PartitionSpec as P

TILE = 128


def contract(left, right):
    return lax.dot_general(
        left, right, (((1,), (1,)), ((), ())), preferred_element_type=jnp.float32
    )


def on_device(amplitudes, integrals, integral_tiles, amplitude_tiles):
    local_rows = amplitudes.shape[0]
    tile_rows = jnp.repeat(amplitude_tiles, TILE, axis=0)
    tile_rows = lax.dynamic_slice_in_dim(
        tile_rows, lax.axis_index("row") * local_rows, local_rows, 0
    )
    amp_mask = jnp.repeat(tile_rows, TILE, axis=1).astype(jnp.bfloat16)
    masked_amps = amplitudes * amp_mask
    int_mask = jnp.repeat(jnp.repeat(integral_tiles, TILE, axis=0), TILE, axis=1).astype(
        jnp.bfloat16
    )
    masked_ints = integrals * int_mask
    panel = lax.all_gather(masked_amps, "row", axis=0, tiled=True)
    return contract(panel, lax.all_gather(masked_ints, "col", axis=1, tiled=True))


def solution(mesh):
    return jax.shard_map(
        on_device,
        mesh=mesh,
        in_specs=(P(("col", "row"), None), P("row", "col"), P("row", "col"), P("col", None)),
        out_specs=P("col", "row"),
        check_vma=False,
    )
```

profile of v0, /device:TPU:0, one launch (start us, length us, event | category | flops | bytes accessed | tf_op | source)
XLA Modules:
  0.0 279.3 jit_solution(6280737660417096425)
XLA Ops:
  6.5 0.0 copy-start.1
  6.5 0.0 all-gather.3.cloned.1.call-start
  6.5 0.7 broadcast_in_dim.12
  7.3 0.6 broadcast_in_dim.13
  7.9 2.8 %bitcast_multiply_fusion.1 = bf16[64,8192]{1,0:T(8,128)(2,1)} fusion(bf16[64,8192]{1,0:T(8,128)(2,1)} %param.4, bf16[8,8,64,128]{3,2,1,0:T(8,128)(2,1)S(1)} %bitcast.11), kind=kLoop, calls=%fused_computation.1 | loop fusion | flops 524288 | bytes 3145728 | tf_op jit(solution)/shard_map/mul | solution.py:22
  10.7 0.0 all-gather.3.cloned.1.call-update
  10.7 0.0 all-gather.5.cloned.1.call-start
  10.8 0.0 copy-done.1
  10.8 0.1 copy.5
  10.9 0.0 copy-start
  10.9 0.1 broadcast_in_dim.14
  11.0 5.8 %broadcast_in_dim.15 = bf16[2048,8,128]{2,1,0:T(8,128)(2,1)S(1)} broadcast(bf16[2048,8]{1,0:T(8,128)(2,1)S(1)} %bitcast.12), dimensions={0,1} | broadcast | bytes 4227072 | tf_op jit(solution)/shard_map/broadcast_in_dim | solution.py:23
  16.8 0.0 copy-done
  16.8 2.5 bitcast_multiply_fusion
  19.3 0.0 all-gather.5.cloned.1.call-update
  19.3 75.1 %all-gather.3.cloned.1.call-done = bf16[256,8192]{1,0:T(8,128)(2,1)} async-done(((bf16[64,8192]{1,0:T(8,128)(2,1)}), bf16[256,8192]{1,0:T(8,128)(2,1)}) %all-gather.3.cloned.1.call-update) | async-done | bytes 4194320 | tf_op jit(solution)/shard_map/all_gather | solution.py:27
  94.3 161.3 %all-gather.5.cloned.1.call-done = bf16[2048,8192]{1,0:T(8,128)(2,1)} async-done(((bf16[2048,1024]{1,0:T(8,128)(2,1)}), bf16[2048,8192]{1,0:T(8,128)(2,1)}) %all-gather.5.cloned.1.call-update) | async-done | bytes 33554448 | tf_op jit(solution)/shard_map/all_gather | solution.py:28
  255.6 16.9 %fusion = f32[256,2048]{1,0:T(8,128)} fusion(bf16[256,8192]{1,0:T(8,128)(2,1)} %all-gather.3.cloned.1.call-done, bf16[2048,8192]{1,0:T(8,128)(2,1)} %all-gather.5.cloned.1.call-done), kind=kOutput, calls=%fused_computation.3 | convolution fusion | flops 8589934592 | bytes 39845888 | tf_op jit(solution)/shard_map/dot_general | solution.py:10
  (2 shorter events, 0.0 us)
Async XLA Ops:
  6.5 4.2 %copy-start.1 = (s32[16,8]{0,1:T(8,128)S(1)}, s32[16,8]{0,1:T(8,128)}, u32[]{:S(2)}) copy-start(s32[16,8]{0,1:T(8,128)} %param.6) | copy-start | bytes 1540
  6.5 87.8 %all-gather.3.cloned.1.call-start = ((), (), s32[]{:S(2)}) async-start(), calls=%async_computation | async-start | bytes 5242880 | tf_op jit(solution)/shard_map/all_gather | solution.py:27
  10.7 244.9 %all-gather.5.cloned.1.call-start = ((), (), s32[]{:S(2)}) async-start(), calls=%async_computation.1 | async-start | bytes 37748736 | tf_op jit(solution)/shard_map/all_gather | solution.py:28
  10.9 5.9 %copy-start = (bf16[2048,1024]{1,0:T(8,128)(2,1)S(1)}, bf16[2048,1024]{1,0:T(8,128)(2,1)}, u32[]{:S(2)}) copy-start(bf16[2048,1024]{1,0:T(8,128)(2,1)} %param.5) | copy-start | bytes 12582916
Sparse Core Ops, SparseCore 0:
  10.8 83.4 all-gather.2
  96.2 159.3 all-gather.4
where the time goes:
time: 280 us; the launch traced here: 279 us
  waiting for transfers between devices  236 us (84%)
  matrix products  16.9 us (6%)
  between operations  13.5 us (5%)
  local copies, waits for them, and re-layouts  7.25 us (3%)
  other arithmetic  5.35 us (2%)
    all_gather x1, waiting for transfers between devices, on_device(): lax.all_gather(masked_ints, 'col', axis=1, tiled=True)  161 us
    all_gather x1, waiting for transfers between devices, on_device(): panel = lax.all_gather(masked_amps, 'row', axis=0, tiled=True)  75.1 us
    dot_general x1, matrix products, contract(): lax.dot_general(left, right, (((1,), (1,)), ((), ())), preferred_element_...  16.9 us
    broadcast_in_dim x1, local copies, waits for them, and re-layouts, on_device(): jnp.repeat(jnp.repeat(integral_tiles, TILE, axis=0), TILE, axis=1)  5.78 us
  transfers between devices with their start and end apart: 2, of which 2 were waited for; matrix products, arithmetic and copies ran while one was open for 3% of the time, Pallas kernels for 0%

commit v1 on v0

--- a/solution.py
+++ b/solution.py
@@ -4,6 +4,19 @@
 from jax.sharding import PartitionSpec as P
 
 TILE = 128
+
+
+def gather_around(x, axis, dim):
+    ways = lax.axis_size(axis)
+    up = [(d, (d + 1) % ways) for d in range(ways)]
+    down = [(d, (d - 1) % ways) for d in range(ways)]
+    earlier, later = ([x], [x])
+    for _ in range(ways // 2):
+        earlier.append(lax.ppermute(earlier[-1], axis, up))
+    for _ in range((ways - 1) // 2):
+        later.append(lax.ppermute(later[-1], axis, down))
+    line = jnp.concatenate([*earlier[::-1], *later[1:]], axis=dim)
+    return jnp.roll(line, (lax.axis_index(axis) - ways // 2) * x.shape[dim], axis=dim)
 
 
 def contract(left, right):
@@ -24,7 +37,7 @@
         jnp.bfloat16
     )
     masked_ints = integrals * int_mask
-    panel = lax.all_gather(masked_amps, "row", axis=0, tiled=True)
+    panel = gather_around(masked_amps, "row", 0)
     return contract(panel, lax.all_gather(masked_ints, "col", axis=1, tiled=True))
 
 

time: 280 us -> 206 us (0.74)
  waiting for transfers between devices: 236 us -> 144 us
  local copies, waits for them, and re-layouts: 7.25 us -> 17.5 us
  starting transfers between devices: 0.04 us -> 6.9 us
    all_gather x1, waiting for transfers between devices: 161 us -> 80.7 us  [on_device(): lax.all_gather(masked_ints, 'col', axis=1, tiled=True)]
    all_gather x1 -> x0, waiting for transfers between devices: 75.1 us -> none  [on_device(): panel = lax.all_gather(masked_amps, 'row', axis=0, tiled=True)]
    ppermute x0 -> x3, waiting for transfers between devices: none -> 63.8 us  [the longest x2 49.4 us: gather_around(): earlier.append(lax.ppermute(earlier[-1], axis, up))]
    unnamed x4 -> x11, local copies, waits for them, and re-layouts: 0.01 us -> 9.86 us
    ppermute x0 -> x3, starting transfers between devices: none -> 6.9 us  [the longest x1 3.82 us: gather_around(): later.append(lax.ppermute(later[-1], axis, down))]
  transfers between devices with their start and end apart: 2 -> 4, of which waited for: 2 -> 4; matrix products, arithmetic and copies ran while one was open for 3% -> 6% of each run, Pallas kernels for 0% -> 0%
where the time goes in v1:
time: 206 us; the launch traced here: 205 us
  waiting for transfers between devices  144 us (70%)
  local copies, waits for them, and re-layouts  17.5 us (8%)
  matrix products  16.9 us (8%)
  between operations  13.5 us (7%)
  starting transfers between devices  6.9 us (3%)
  other arithmetic  6.14 us (3%)
    all_gather x1, waiting for transfers between devices, on_device(): lax.all_gather(masked_ints, 'col', axis=1, tiled=True)  80.7 us
    ppermute x2, waiting for transfers between devices, gather_around(): earlier.append(lax.ppermute(earlier[-1], axis, up))  49.4 us
    dot_general x1, matrix products, contract(): lax.dot_general(left, right, (((1,), (1,)), ((), ())), preferred_element_...  16.9 us
    ppermute x1, waiting for transfers between devices, gather_around(): later.append(lax.ppermute(later[-1], axis, down))  14.4 us
    unnamed x11, local copies, waits for them, and re-layouts  9.86 us
    broadcast_in_dim x1, local copies, waits for them, and re-layouts, on_device(): jnp.repeat(jnp.repeat(integral_tiles, TILE, axis=0), TILE, axis=1)  5.78 us
    mul x1, other arithmetic, on_device(): masked_ints = integrals * int_mask  4.75 us
  transfers between devices with their start and end apart: 4, of which 4 were waited for; matrix products, arithmetic and copies ran while one was open for 6% of the time, Pallas kernels for 0%

profile of v1, /device:TPU:0, one launch (start us, length us, event | category | flops | bytes accessed | tf_op | source)
XLA Modules:
  0.0 205.4 jit_solution(5551393202494412385)
XLA Ops:
  6.5 0.0 all-gather.2.cloned.1.call-start
  6.5 0.7 convert_element_type.20
  7.2 0.1 copy.5
  7.3 0.1 broadcast_in_dim.14
  7.4 5.8 %broadcast_in_dim.15 = bf16[2048,8,128]{2,1,0:T(8,128)(2,1)S(1)} broadcast(bf16[2048,8]{1,0:T(8,128)(2,1)S(1)} %bitcast.11), dimensions={0,1} | broadcast | bytes 4227072 | tf_op jit(solution)/shard_map/broadcast_in_dim | solution.py:36
  13.2 0.0 copy-start.1
  13.2 0.0 copy-start
  13.2 4.8 %bitcast_multiply_fusion = bf16[2048,1024]{1,0:T(8,128)(2,1)} fusion(bf16[2048,1024]{1,0:T(8,128)(2,1)} %param.5, bf16[256,8,8,128]{3,2,1,0:T(8,128)(2,1)S(1)} %bitcast.9), kind=kLoop, calls=%fused_computation | loop fusion | flops 2097152 | bytes 12582912 | tf_op jit(solution)/shard_map/mul | solution.py:39
  18.0 0.0 all-gather.2.cloned.1.call-update
  18.0 0.0 copy-done.1
  18.0 0.6 broadcast_in_dim.13
  18.6 0.0 copy-done
  18.7 0.7 bitcast_multiply_fusion.1
  19.4 3.1 %collective-permute-start = (bf16[64,8192]{1,0:T(8,128)(2,1)S(1)}, bf16[64,8192]{1,0:T(8,128)(2,1)S(1)}, u32[]{:S(2)}, u32[]{:S(2)}) collective-permute-start(bf16[64,8192]{1,0:T(8,128)(2,1)S(1)} %bitcast_multiply_fusion.1), channel_id=1, source_target_pairs={{0,8},{8,16},{16,24},{24,0},{1,9},{9,17},{17,25},{25,1},{2,10},{10... | collective-permute-start | bytes 3145736 | tf_op jit(solution)/shard_map/ppermute | solution.py:15
  22.4 25.2 %collective-permute-done = bf16[64,8192]{1,0:T(8,128)(2,1)S(1)} collective-permute-done((bf16[64,8192]{1,0:T(8,128)(2,1)S(1)}, bf16[64,8192]{1,0:T(8,128)(2,1)S(1)}, u32[]{:S(2)}, u32[]{:S(2)}) %collective-permute-start) | collective-permute-done | bytes 1048608 | tf_op jit(solution)/shard_map/ppermute | solution.py:15
  47.6 0.0 collective-permute-start.1
  47.6 3.8 %collective-permute-start.2 = (bf16[64,8192]{1,0:T(8,128)(2,1)S(1)}, bf16[64,8192]{1,0:T(8,128)(2,1)S(1)}, u32[]{:S(2)}, u32[]{:S(2)}) collective-permute-start(bf16[64,8192]{1,0:T(8,128)(2,1)S(1)} %bitcast_multiply_fusion.1), channel_id=1, source_target_pairs={{0,24},{8,0},{16,8},{24,16},{1,25},{9,1},{17,9},{25,17},{2,26},{10... | collective-permute-start | bytes 3145736 | tf_op jit(solution)/shard_map/ppermute | solution.py:17
  51.4 24.2 %collective-permute-done.1 = bf16[64,8192]{1,0:T(8,128)(2,1)} collective-permute-done((bf16[64,8192]{1,0:T(8,128)(2,1)S(1)}, bf16[64,8192]{1,0:T(8,128)(2,1)}, u32[]{:S(2)}, u32[]{:S(2)}) %collective-permute-start.1) | collective-permute-done | bytes 1048608 | tf_op jit(solution)/shard_map/ppermute | solution.py:15
  75.6 2.3 %constant_dynamic-update-slice_fusion.7 = bf16[512,8192]{1,0:T(8,128)(2,1)} fusion(bf16[64,8192]{1,0:T(8,128)(2,1)} %collective-permute-done.1), kind=kLoop, calls=%fused_computation.12 | loop fusion | bytes 2097152
  77.9 1.1 constant_dynamic-update-slice_fusion.6
  79.0 1.0 constant_dynamic-update-slice_fusion.5
  80.0 14.4 %collective-permute-done.2 = bf16[64,8192]{1,0:T(8,128)(2,1)S(1)} collective-permute-done((bf16[64,8192]{1,0:T(8,128)(2,1)S(1)}, bf16[64,8192]{1,0:T(8,128)(2,1)S(1)}, u32[]{:S(2)}, u32[]{:S(2)}) %collective-permute-start.2) | collective-permute-done | bytes 1048608 | tf_op jit(solution)/shard_map/ppermute | solution.py:17
  94.4 1.1 constant_dynamic-update-slice_fusion.4
  95.5 2.3 %constant_dynamic-update-slice_fusion.3 = bf16[512,8192]{1,0:T(8,128)(2,1)} fusion(bf16[512,8192]{1,0:T(8,128)(2,1)} %constant_dynamic-update-slice_fusion.4, bf16[64,8192]{1,0:T(8,128)(2,1)} %collective-permute-done.1), kind=kLoop, calls=%fused_computation.8 | loop fusion | bytes 2097152
  97.8 1.0 constant_dynamic-update-slice_fusion.2
  98.8 1.1 constant_dynamic-update-slice_fusion.1
  99.9 1.1 constant_dynamic-update-slice_fusion
  101.0 80.7 %all-gather.2.cloned.1.call-done = bf16[2048,8192]{1,0:T(8,128)(2,1)} async-done(((bf16[2048,1024]{1,0:T(8,128)(2,1)}), bf16[2048,8192]{1,0:T(8,128)(2,1)}) %all-gather.2.cloned.1.call-update) | async-done | bytes 33554448 | tf_op jit(solution)/shard_map/all_gather | solution.py:41
  181.6 16.9 %fusion = f32[256,2048]{1,0:T(8,128)} fusion(bf16[2048,8192]{1,0:T(8,128)(2,1)} %all-gather.2.cloned.1.call-done, bf16[512,8192]{1,0:T(8,128)(2,1)} %constant_dynamic-update-slice_fusion, s32[]{:T(128)S(6)} %select_n.18), kind=kOutput, calls=%fused_computation.1 | convolution fusion | flops 8589934592 | bytes 39845892 | tf_op jit(solution)/shard_map/dot_general | solution.py:23
  (2 shorter events, 0.0 us)
Async XLA Ops:
  6.5 175.1 %all-gather.2.cloned.1.call-start = ((), (), s32[]{:S(2)}) async-start(), calls=%async_computation | async-start | bytes 37748736 | tf_op jit(solution)/shard_map/all_gather | solution.py:41
  13.2 4.8 %copy-start.1 = (s32[2,64]{1,0:T(2,128)S(1)}, s32[2,64]{1,0:T(2,128)}, u32[]{:S(2)}) copy-start(s32[2,64]{1,0:T(2,128)} %param.7) | copy-start | bytes 1540
  13.2 5.5 %copy-start = (bf16[64,8192]{1,0:T(8,128)(2,1)S(1)}, bf16[64,8192]{1,0:T(8,128)(2,1)}, u32[]{:S(2)}) copy-start(bf16[64,8192]{1,0:T(8,128)(2,1)} %param.4) | copy-start | bytes 3145732
  19.4 28.3 %collective-permute-start = (bf16[64,8192]{1,0:T(8,128)(2,1)S(1)}, bf16[64,8192]{1,0:T(8,128)(2,1)S(1)}, u32[]{:S(2)}, u32[]{:S(2)}) collective-permute-start(bf16[64,8192]{1,0:T(8,128)(2,1)S(1)} %bitcast_multiply_fusion.1), channel_id=1, source_target_pairs={{0,8},{8,16},{16,24},{24,0},{1,9},{9,17},{17,25},{25,1},{2,10},{10... | collective-permute-start | bytes 3145736 | tf_op jit(solution)/shard_map/ppermute | solution.py:15
  47.6 28.0 %collective-permute-start.1 = (bf16[64,8192]{1,0:T(8,128)(2,1)S(1)}, bf16[64,8192]{1,0:T(8,128)(2,1)}, u32[]{:S(2)}, u32[]{:S(2)}) collective-permute-start(bf16[64,8192]{1,0:T(8,128)(2,1)S(1)} %collective-permute-done), channel_id=1, source_target_pairs={{0,8},{8,16},{16,24},{24,0},{1,9},{9,17},{17,25},{25,1},{2,10},{10... | collective-permute-start | bytes 3145736 | tf_op jit(solution)/shard_map/ppermute | solution.py:15
  47.6 46.8 %collective-permute-start.2 = (bf16[64,8192]{1,0:T(8,128)(2,1)S(1)}, bf16[64,8192]{1,0:T(8,128)(2,1)S(1)}, u32[]{:S(2)}, u32[]{:S(2)}) collective-permute-start(bf16[64,8192]{1,0:T(8,128)(2,1)S(1)} %bitcast_multiply_fusion.1), channel_id=1, source_target_pairs={{0,24},{8,0},{16,8},{24,16},{1,25},{9,1},{17,9},{25,17},{2,26},{10... | collective-permute-start | bytes 3145736 | tf_op jit(solution)/shard_map/ppermute | solution.py:17
Sparse Core Ops, SparseCore 0:
  18.1 163.4 all-gather.1
